TPU v7x, 256 devices: a whole 4x4x8 slice. The times are simulated.
256 devices in a mesh: ctx: 4 (over y), row: 4 (over x_hi, core), col: 16 (over x_lo, z).
Axes of the slice: x: 4 (x_hi: 2, x_lo: 2; x = x_hi * 2 + x_lo), y: 4, z: 8, core: 2. Of those that a mesh axis runs over, the one named last changes fastest.
Arguments:
- events: bfloat16 [8192, 4096], P(('ctx', 'row'), 'col'), may hold values from -120 to 120
- domain_ids: int32 [8192], P(('ctx', 'row')), may hold values from 0 to 3
- block_order: int32 [4], replicated, may hold values from 0 to 3, each once
- query_weight: bfloat16 [4096, 4096], P('row', 'col'), may hold values from -0.09375 to 0.09375
- keyval_weight: bfloat16 [4096, 8, 2, 128], P('row'), may hold values from -0.09375 to 0.09375
- head_bias: float32 [32], P('col'), may hold values from -1.5 to 1.5
- out_weight: bfloat16 [4096, 4096], P('row', 'col'), may hold values from -0.09375 to 0.09375
Outputs:
- mixed: bfloat16 [8192, 4096], P(('ctx', 'row'), 'col')
Inputs may be any that keep to these rules, and one draw needn't show every extreme that they name: `block_order`: each index of ctx holds 2048 consecutive events of one block; every place 0 to 3 is named once.
All inputs are finite; a program needn't handle non-finite values.
Results may differ from a plain program's by a relative error of at most 0.0075.
Values may be sent and summed in bfloat16 or wider, within the bound.
No kernel may reach another device: no remote copies, remote signals or barrier semaphores. Data moves between devices by JAX's collectives and lax.ppermute only.
A program may use at most 128 MiB of HBM per device.

v0:
```python
import math
import jax
import jax.numpy as jnp
from jax import lax
from jax.sharding import Mesh
from jax.sharding import PartitionSpec as P

H = 32
KV = 8
HD = 128
COL = ("col_0", "col_1")
norm_eps = 1e-06
block_rows = 512


def in_order(blocks, dim):
    dims = list(blocks.shape[1:])
    dims[dim] *= blocks.shape[0]
    return jnp.moveaxis(blocks, 0, dim).reshape(dims)


def gather_in_order(shard, axes, sequence):
    blocks = shard[None]
    for k in sequence:
        blocks = lax.all_gather(blocks, axes[k], axis=0, tiled=True)
    current = [lax.axis_size(axes[k]) for k in reversed(sequence)]
    blocks = blocks.reshape(*current, *shard.shape)
    turned = sorted(range(len(sequence)), key=lambda place: sequence[len(sequence) - 1 - place])
    return blocks.transpose(*turned, *range(len(sequence), blocks.ndim)).reshape(-1, *shard.shape)


def gather_axes(shard, axes, sequence, dim):
    return in_order(gather_in_order(shard, axes, sequence), dim)


def side_by_side(arrays, axis, dim, along):
    both = jnp.concatenate(arrays, axis=along)
    filled, at, outs = (lax.all_gather(both, axis, axis=dim, tiled=True), 0, [])
    for a in arrays:
        outs.append(lax.slice_in_dim(filled, at, at + a.shape[along], axis=along))
        at += a.shape[along]
    return tuple(outs)


def sent_to_all(shard, axis):
    devices = lax.axis_size(axis)
    return lax.all_to_all(
        jnp.broadcast_to(shard[None], (devices, *shard.shape)), axis, 0, 0, tiled=True
    )


def collect(shard, axis, dim):
    return in_order(sent_to_all(shard, axis), dim)


def block_place(storage, group_rows, block_order):
    block_index = storage // group_rows
    choices_row = jnp.arange(block_order.shape[0], dtype=jnp.int32)
    looked_up = jnp.sum(
        jnp.where(block_index[:, None] == choices_row[None, :], block_order[None, :], 0), axis=1
    )
    return looked_up * group_rows + storage % group_rows


def shards(events, domain_ids, block_order, query_weight, keyval_weight, head_bias, out_weight):
    row_count = events.shape[0]
    head_count = head_bias.shape[0]
    group_size = H // KV
    pair_heads = max(1, head_count // group_size)
    group_heads = head_count // pair_heads
    group_rows = row_count * lax.axis_size("row")
    scale_factor = 1.0 / math.sqrt(HD)
    whole = gather_axes(events, COL, (0, 1), 1)
    wide_events = whole.astype(jnp.float32)
    normed = (
        wide_events
        * lax.rsqrt(jnp.mean(wide_events * wide_events, axis=1, keepdims=True) + norm_eps)
    ).astype(jnp.bfloat16)
    pair_start = lax.axis_index(COL) * head_count // group_size
    pair_weight = lax.dynamic_slice_in_dim(keyval_weight, pair_start, pair_heads, 1)
    pair_weight = pair_weight.reshape(keyval_weight.shape[0], pair_heads * 2 * HD)
    portions = side_by_side((query_weight, pair_weight), "row", 0, 1)
    columns = normed
    query_sums = jnp.dot(columns, portions[0], preferred_element_type=jnp.float32)
    pair_sums = jnp.dot(columns, portions[1], preferred_element_type=jnp.float32)
    queries = query_sums.astype(jnp.bfloat16).reshape(row_count, pair_heads, group_heads, HD)
    keyvals = pair_sums.astype(jnp.bfloat16).reshape(row_count, pair_heads, 2, HD)
    first_row = (lax.axis_index("ctx") * lax.axis_size("row") + lax.axis_index("row")) * row_count
    query_place = block_place(
        first_row + jnp.arange(row_count, dtype=jnp.int32), group_rows, block_order
    )
    inv_count = lax.rsqrt((query_place + 1).astype(jnp.float32))
    head_terms = head_bias.reshape(pair_heads, group_heads)

    def compute_block(running, kv_block, domain_block, key_place):
        scores = (
            jnp.einsum(
                "qkgd,nkd->kgqn", queries, kv_block[:, :, 0, :], preferred_element_type=jnp.float32
            )
            * scale_factor
        )
        same_domain = (domain_ids[:, None] == domain_block[None, :]).astype(jnp.float32)
        scores = scores + head_terms[:, :, None, None] * same_domain[None, None, :, :]
        visible = key_place[None, :] <= query_place[:, None]
        weights = jnp.where(
            visible[None, None, :, :], jax.nn.silu(scores) * inv_count[None, None, :, None], 0.0
        ).astype(jnp.bfloat16)
        return running + jnp.einsum(
            "kgqn,nkd->qkgd", weights, kv_block[:, :, 1, :], preferred_element_type=jnp.float32
        )

    def update(running, kv_block, domain_block, block_first):
        key_place = block_place(
            block_first + jnp.arange(kv_block.shape[0], dtype=jnp.int32), group_rows, block_order
        )
        return compute_block(running, kv_block, domain_block, key_place)

    empty_sums = jnp.zeros((row_count, pair_heads, group_heads, HD), jnp.float32)
    totals = empty_sums
    kv_part = lax.all_gather(keyvals, ("ctx", "row"), axis=0, tiled=True)
    domain_part = lax.all_gather(domain_ids, ("ctx", "row"), axis=0, tiled=True)
    length_rows = kv_part.shape[0]
    number = length_rows // block_rows
    kv_blocks = kv_part.reshape((number, block_rows) + kv_part.shape[1:])
    domain_blocks = domain_part.reshape(number, block_rows)
    firsts = block_rows * jnp.arange(number, dtype=jnp.int32)

    def scan_step(running, block_item):
        return (update(running, block_item[0], block_item[1], block_item[2]), None)

    totals, unused = lax.scan(scan_step, totals, (kv_blocks, domain_blocks, firsts))
    attended = totals
    attended = attended.astype(jnp.bfloat16).reshape(row_count, head_count * HD)
    all_heads = lax.all_gather(attended, COL, axis=1, tiled=True)
    columns = all_heads
    out_sums = jnp.dot(columns, collect(out_weight, "row", 0), preferred_element_type=jnp.float32)
    return out_sums.astype(jnp.bfloat16)


def solution(mesh):
    split = Mesh(
        mesh.devices.reshape(mesh.shape["ctx"], mesh.shape["row"], 2, 8),
        ("ctx", "row", "col_0", "col_1"),
    )
    return jax.shard_map(
        shards,
        mesh=split,
        in_specs=(
            P(("ctx", "row"), COL),
            P(("ctx", "row")),
            P(),
            P("row", COL),
            P("row", None, None, None),
            P(COL),
            P("row", COL),
        ),
        out_specs=P(("ctx", "row"), COL),
        check_vma=False,
    )
```

profile of v0, /device:TPU:8, one launch (start us, length us, event | category | flops | bytes accessed | tf_op | source)
XLA Modules:
  0.0 338.7 jit_solution(12113207221270040131)
XLA Ops:
  6.5 10.4 %all-gather = bf16[1024,256]{1,0:T(8,128)(2,1)} all-gather(bf16[512,256]{1,0:T(8,128)(2,1)} %param.9), channel_id=2, replica_groups=mesh['ctx'=4,'row'=4,'col_0'=2,'col_1'=8] {'col_0'}, dimensions={0}, use_global_device_ids=true | all-gather | bytes 786432 | tf_op jit(solution)/shard_map/all_gather | solution.py:25
  17.0 1.4 constant_dynamic-slice_fusion.1
  18.6 2.2 pad_maximum_fusion
  20.8 53.7 %all-gather.7.cloned.1.call-done = bf16[16,512,256]{2,1,0:T(8,128)(2,1)} async-done(((bf16[2,512,256]{2,1,0:T(8,128)(2,1)}), bf16[16,512,256]{2,1,0:T(8,128)(2,1)}) %all-gather.7.cloned.1.call-update) | async-done | bytes 4194320 | tf_op jit(solution)/shard_map/all_gather | solution.py:25
  74.5 3.1 convert_bitcast_fusion
  77.6 3.8 %copy.33 = f32[2,8,512,256]{3,2,1,0:T(8,128)} copy(f32[2,8,512,256]{3,2,0,1:T(8,128)S(1)} %convert_bitcast_fusion) | data formatting | bytes 16777216 | tf_op jit(solution)/shard_map/convert_element_type | solution.py:74
  81.4 9.4 %copy.34 = f32[512,16,256]{0,2,1:T(8,128)} copy(f32[512,16,256]{2,0,1:T(8,128)} %bitcast.98) | data formatting | bytes 16777216 | tf_op jit(solution)/shard_map/convert_element_type | solution.py:74
  90.8 3.1 fusion.20
  93.9 6.6 %fusion.21 = bf16[512,4096]{0,1:T(8,128)(2,1)} fusion(f32[512,16,256]{0,2,1:T(8,128)} %copy.34, f32[512]{0:T(512)S(1)} %add_rsqrt_fusion), kind=kLoop, calls=%fused_computation.40 | loop fusion | flops 4194304 | bytes 12584960 | tf_op jit(solution)/shard_map/convert_element_type | solution.py:78
  100.5 15.5 %all-gather.9.cloned.1.call-done = bf16[4096,512]{1,0:T(8,128)(2,1)} async-done(((bf16[1024,512]{1,0:T(8,128)(2,1)}), bf16[4096,512]{1,0:T(8,128)(2,1)}) %all-gather.9.cloned.1.call-update) | async-done | bytes 4194320 | tf_op jit(solution)/shard_map/all_gather | solution.py:38
  116.0 4.2 %fusion.26 = bf16[512,256]{0,1:T(8,128)(2,1)S(1)} fusion(bf16[512,4096]{0,1:T(8,128)(2,1)} %fusion.21, bf16[4096,512]{1,0:T(8,128)(2,1)} %all-gather.9.cloned.1.call-done), kind=kOutput, calls=%fused_computation.45 | convolution fusion | flops 1073872896 | bytes 6553600 | tf_op jit(solution)/shard_map/dot_general | solution.py:85
  121.1 19.7 %all-gather.1 = s32[16,1,512]{2,1,0:T(1,128)S(1)} all-gather(s32[1,1,512]{2,1,0:T(1,128)S(1)} %bitcast.109), channel_id=1, replica_groups=mesh['ctx'=4,'row'=4,'col_0'=2,'col_1'=8] {'ctx','row'}, dimensions={0}, use_global_device_ids=true | all-gather | bytes 34816 | tf_op jit(solution)/shard_map/all_gather | solution.py:121
  140.9 4.2 %fusion.29 = bf16[512,256]{0,1:T(8,128)(2,1)S(1)} fusion(bf16[512,4096]{0,1:T(8,128)(2,1)} %fusion.21, bf16[4096,512]{1,0:T(8,128)(2,1)} %all-gather.9.cloned.1.call-done), kind=kOutput, calls=%fused_computation.46 | convolution fusion | flops 1073872896 | bytes 6553600 | tf_op jit(solution)/shard_map/dot_general | solution.py:84
  145.3 34.0 %all-gather.11.cloned.1.call-done = bf16[8192,1,2,128]{3,0,2,1:T(8,128)(2,1)} async-done(((bf16[512,1,2,128]{3,0,2,1:T(8,128)(2,1)}), bf16[8192,1,2,128]{3,0,2,1:T(8,128)(2,1)}) %all-gather.11.cloned.1.call-update) | async-done | bytes 4194320 | tf_op jit(solution)/shard_map/all_gather | solution.py:120
  179.2 72.2 %while.13 = (s32[]{:T(128)}, f32[512,1,2,128]{0,3,2,1:T(8,128)S(1)}, bf16[16,512,1,2,128]{4,1,0,3,2:T(8,128)(2,1)}, s32[16]{0:T(128)S(1)}, s32[4]{0:T(128)S(1)},...) while((s32[]{:T(128)}, ...), condition=%wide.region_4.5_spmd.clone, body=%wide.region_2.4_spmd.clone.sunk | while | flops 274747904 | bytes 4743363 | solution.py:131
  182.5 1.2 fusion.46
  191.6 1.2 fusion.46
  196.1 1.2 fusion.46
  200.6 1.2 fusion.46
  205.1 1.2 fusion.46
  209.6 1.2 fusion.46
  214.1 1.2 fusion.46
  218.6 1.2 fusion.46
  223.1 1.2 fusion.46
  227.7 1.2 fusion.46
  232.2 1.2 fusion.46
  236.7 1.2 fusion.46
  245.7 1.2 fusion.46
  250.2 1.2 fusion.46
  252.4 69.7 %all_to_all.5 = bf16[4,1024,256]{2,1,0:T(8,128)(2,1)S(1)} all-to-all(bf16[4,1024,256]{2,1,0:T(8,128)(2,1)S(1)} %broadcast_in_dim.74), channel_id=1, replica_groups=mesh['ctx'=4,'row'=4,'col_0'=2,'col_1'=8] {'row'}, dimensions={0} | all-to-all | bytes 4194304 | tf_op jit(solution)/shard_map/all_to_all | solution.py:47
  322.0 6.0 %all-gather.13.cloned.1.call-done = bf16[512,4096]{0,1:T(8,128)(2,1)} async-done(((bf16[512,256]{0,1:T(8,128)(2,1)}), bf16[512,4096]{0,1:T(8,128)(2,1)}) %all-gather.13.cloned.1.call-update) | async-done | bytes 4194320 | tf_op jit(solution)/shard_map/all_gather | solution.py:134
  328.0 4.2 %convolution_convert_fusion = bf16[512,256]{1,0:T(8,128)(2,1)} fusion(bf16[512,4096]{0,1:T(8,128)(2,1)} %all-gather.13.cloned.1.call-done, bf16[4096,256]{1,0:T(8,128)(2,1)S(1)} %bitcast.100), kind=kOutput, calls=%fused_computation.47 | convolution fusion | flops 1073872896 | bytes 6553600 | tf_op jit(solution)/shard_map/dot_general | solution.py:136
  (142 shorter events, 56.7 us)
Async XLA Ops:
  6.5 67.9 %all-gather.7.cloned.1.call-start = ((), (), s32[]{:S(2)}) async-start(), calls=%async_computation.1 | async-start | bytes 4718592 | tf_op jit(solution)/shard_map/all_gather | solution.py:25
  17.0 99.0 %all-gather.9.cloned.1.call-start = ((), (), s32[]{:S(2)}) async-start(), calls=%async_computation.2 | async-start | bytes 5242880 | tf_op jit(solution)/shard_map/all_gather | solution.py:38
  20.8 158.5 %all-gather.11.cloned.1.call-start = ((), (), s32[]{:S(2)}) async-start(), calls=%async_computation.3 | async-start | bytes 4456448 | tf_op jit(solution)/shard_map/all_gather | solution.py:120
  100.5 20.6 %copy-start.1 = (s32[512]{0:T(512)S(1)}, s32[512]{0:T(512)}, u32[]{:S(2)}) copy-start(s32[512]{0:T(512)} %param.10) | copy-start | bytes 6148
  100.5 40.3 %copy-start.2 = (s32[4]{0:T(128)S(1)}, s32[4]{0:T(128)}, u32[]{:S(2)}) copy-start(s32[4]{0:T(128)} %param.11) | copy-start | bytes 52
  121.0 207.0 %all-gather.13.cloned.1.call-start = ((), (), s32[]{:S(2)}) async-start(), calls=%async_computation.4 | async-start | bytes 4456448 | tf_op jit(solution)/shard_map/all_gather | solution.py:134
  140.9 38.4 %copy-start.3 = (f32[2]{0:T(128)S(1)}, f32[2]{0:T(128)}, u32[]{:S(2)}) copy-start(f32[2]{0:T(128)} %param.14) | copy-start | bytes 28
  179.2 73.0 %copy-start = (bf16[1024,256]{1,0:T(8,128)(2,1)S(1)}, bf16[1024,256]{1,0:T(8,128)(2,1)}, u32[]{:S(2)}) copy-start(bf16[1024,256]{1,0:T(8,128)(2,1)} %param.15) | copy-start | bytes 1572868
Sparse Core Ops, SparseCore 0:
  17.1 57.3 all-gather.6
  76.3 39.6 all-gather.8
  121.1 58.0 all-gather.10
  252.3 75.6 all-gather.12
where the time goes:
time: 340 us; the launch traced here: 339 us
  waiting for transfers between devices  109 us (32%)
  blocking collectives  99.8 us (29%)
  other arithmetic  42.6 us (13%)
  local copies, waits for them, and re-layouts  41.1 us (12%)
  matrix products  31.9 us (9%)
  between operations  13.3 us (4%)
    all_to_all x1, blocking collectives, sent_to_all(): lax.all_to_all(jnp.broadcast_to(shard[None], (devices, *shard.shape)), ax...  69.7 us
    all_gather x1, waiting for transfers between devices, gather_in_order(): blocks = lax.all_gather(blocks, axes[k], axis=0, tiled=True)  53.7 us
    all_gather x1, waiting for transfers between devices, shards(): kv_part = lax.all_gather(keyvals, ('ctx', 'row'), axis=0, tiled=True)  34 us
    all_gather x1, blocking collectives, shards(): domain_part = lax.all_gather(domain_ids, ('ctx', 'row'), axis=0, tiled=True)  19.7 us
    dot_general x16, matrix products, compute_block(): jnp.einsum('kgqn,nkd->qkgd', weights, kv_block[:, :, 1, :], preferred_ele...  19.3 us
    squeeze x16, local copies, waits for them, and re-layouts, shards(): lax.scan(scan_step, totals, (kv_blocks, domain_blocks, firsts))  15.6 us
    all_gather x1, waiting for transfers between devices, side_by_side(): filled, at, outs = (lax.all_gather(both, axis, axis=dim, tiled=True), 0, [])  15.5 us
    convert_element_type x2, local copies, waits for them, and re-layouts, shards(): wide_events = whole.astype(jnp.float32)  13.2 us
  transfers between devices with their start and end apart: 4, of which 4 were waited for; matrix products, arithmetic and copies ran while one was open for 10% of the time, Pallas kernels for 0%

commit v1 on v0

--- a/solution.py
+++ b/solution.py
@@ -22,7 +22,10 @@
 def gather_in_order(shard, axes, sequence):
     blocks = shard[None]
     for k in sequence:
-        blocks = lax.all_gather(blocks, axes[k], axis=0, tiled=True)
+        v0 = axes[k]
+        blocks = jnp.concatenate(
+            lax.all_to_all(jnp.stack([blocks for _ in range(lax.psum(1, v0))], axis=0), v0, 0, 0), 0
+        )
     current = [lax.axis_size(axes[k]) for k in reversed(sequence)]
     blocks = blocks.reshape(*current, *shard.shape)
     turned = sorted(range(len(sequence)), key=lambda place: sequence[len(sequence) - 1 - place])

time: 340 us -> 371 us (1.091)
  waiting for transfers between devices: 109 us -> 127 us
  starting transfers between devices: 0.13 us -> 8.72 us
    all_to_all x0 -> x1, waiting for transfers between devices: none -> 92.6 us  [gather_in_order(): lax.all_to_all(jnp.stack([blocks for _ in range(lax.psum(1, v0))], axis=0...]
    all_gather x1 -> x0, waiting for transfers between devices: 53.7 us -> none  [gather_in_order(): blocks = lax.all_gather(blocks, axes[k], axis=0, tiled=True)]
    all_gather x1, waiting for transfers between devices: 15.5 us -> 0.01 us  [side_by_side(): filled, at, outs = (lax.all_gather(both, axis, axis=dim, tiled=True), 0, [])]
    all_to_all x0 -> x1, blocking collectives: none -> 10.7 us  [gather_in_order(): lax.all_to_all(jnp.stack([blocks for _ in range(lax.psum(1, v0))], axis=0...]
    all_gather x1 -> x0, blocking collectives: 10.4 us -> none  [gather_in_order(): blocks = lax.all_gather(blocks, axes[k], axis=0, tiled=True)]
    all_to_all x0 -> x1, starting transfers between devices: none -> 8.6 us  [gather_in_order(): lax.all_to_all(jnp.stack([blocks for _ in range(lax.psum(1, v0))], axis=0...]
    all_gather x1, waiting for transfers between devices: 34 us -> 28 us  [shards(): kv_part = lax.all_gather(keyvals, ('ctx', 'row'), axis=0, tiled=True)]
    convert_element_type x2 -> x1, local copies, waits for them, and re-layouts: 13.2 us -> 9.27 us  [shards(): wide_events = whole.astype(jnp.float32)]
  transfers between devices with their start and end apart: 4 -> 4, of which waited for: 4 -> 3; matrix products, arithmetic and copies ran while one was open for 10% -> 9% of each run, Pallas kernels for 0% -> 0%
where the time goes in v1:
time: 371 us; the launch traced here: 370 us
  waiting for transfers between devices  127 us (34%)
  blocking collectives  102 us (27%)
  other arithmetic  45.8 us (12%)
  local copies, waits for them, and re-layouts  39.5 us (11%)
  matrix products  31.9 us (9%)
  between operations  13.3 us (4%)
  starting transfers between devices  8.72 us (2%)
    all_to_all x1, waiting for transfers between devices, gather_in_order(): lax.all_to_all(jnp.stack([blocks for _ in range(lax.psum(1, v0))], axis=0...  92.6 us
    all_to_all x1, blocking collectives, sent_to_all(): lax.all_to_all(jnp.broadcast_to(shard[None], (devices, *shard.shape)), ax...  69 us
    all_gather x1, waiting for transfers between devices, shards(): kv_part = lax.all_gather(keyvals, ('ctx', 'row'), axis=0, tiled=True)  28 us
    all_gather x1, blocking collectives, shards(): domain_part = lax.all_gather(domain_ids, ('ctx', 'row'), axis=0, tiled=True)  22.5 us
    dot_general x16, matrix products, compute_block(): jnp.einsum('kgqn,nkd->qkgd', weights, kv_block[:, :, 1, :], preferred_ele...  19.3 us
    squeeze x16, local copies, waits for them, and re-layouts, shards(): lax.scan(scan_step, totals, (kv_blocks, domain_blocks, firsts))  15.6 us
    all_to_all x1, blocking collectives, gather_in_order(): lax.all_to_all(jnp.stack([blocks for _ in range(lax.psum(1, v0))], axis=0...  10.7 us
    add x16, other arithmetic, block_place(): return looked_up * group_rows + storage % group_rows  10.5 us
  transfers between devices with their start and end apart: 4, of which 3 were waited for; matrix products, arithmetic and copies ran while one was open for 9% of the time, Pallas kernels for 0%

profile of v1, /device:TPU:8, one launch (start us, length us, event | category | flops | bytes accessed | tf_op | source)
XLA Modules:
  0.0 369.6 jit_solution(17799268287294653943)
XLA Ops:
  7.6 10.7 %all_to_all.15 = bf16[2,1,512,256]{3,2,1,0:T(8,128)(2,1)S(1)} all-to-all(bf16[2,1,512,256]{3,2,1,0:T(8,128)(2,1)S(1)} %pad_maximum_fusion.1), channel_id=1, replica_groups=mesh['ctx'=4,'row'=4,'col_0'=2,'col_1'=8] {'col_0'}, dimensions={0} | all-to-all | bytes 1048576 | tf_op jit(solution)/shard_map/all_to_all | solution.py:27
  18.3 2.4 stack.7
  20.6 8.6 %all-to-all-start.1 = ((bf16[8,2,512,256]{3,2,1,0:T(8,128)(2,1)}), bf16[8,2,512,256]{3,2,1,0:T(8,128)(2,1)}, u32[]{:S(2)}, u32[]{:S(2)}) async-start(bf16[8,2,512,256]{3,2,1,0:T(8,128)(2,1)} %stack.7), calls=%async_computation.1 | async-start | bytes 8388608 | tf_op jit(solution)/shard_map/all_to_all | solution.py:27
  29.3 1.4 constant_dynamic-slice_fusion.1
  32.0 92.6 %all-to-all-done.1 = bf16[8,2,512,256]{3,2,1,0:T(8,128)(2,1)} async-done(((bf16[8,2,512,256]{3,2,1,0:T(8,128)(2,1)}), bf16[8,2,512,256]{3,2,1,0:T(8,128)(2,1)}, u32[]{:S(2)}, u32[]{:S(2)}) %all-to-all-start.1) | async-done | bytes 4194336 | tf_op jit(solution)/shard_map/all_to_all | solution.py:27
  124.7 6.3 %copy_convert_fusion = f32[8,2,512,256]{3,2,0,1:T(8,128)} fusion(bf16[8,2,512,256]{3,2,1,0:T(8,128)(2,1)} %all-to-all-done.1), kind=kLoop, calls=%fused_computation.39 | loop fusion | flops 2097152 | bytes 12582912 | tf_op jit(solution)/shard_map/convert_element_type | solution.py:77
  131.0 9.3 %copy.27 = f32[512,16,256]{0,2,1:T(8,128)} copy(f32[512,16,256]{2,0,1:T(8,128)} %bitcast.96) | data formatting | bytes 16777216 | tf_op jit(solution)/shard_map/convert_element_type | solution.py:77
  140.3 3.1 multiply_reduce_fusion
  143.4 6.5 %fusion.20 = bf16[512,4096]{0,1:T(8,128)(2,1)} fusion(f32[512,16,256]{0,2,1:T(8,128)} %copy.27, f32[512]{0:T(512)S(1)} %add_rsqrt_fusion), kind=kLoop, calls=%fused_computation.37 | loop fusion | flops 4194304 | bytes 12584960 | tf_op jit(solution)/shard_map/convert_element_type | solution.py:81
  149.9 4.2 %fusion.25 = bf16[512,256]{0,1:T(8,128)(2,1)S(1)} fusion(bf16[512,4096]{0,1:T(8,128)(2,1)} %fusion.20, bf16[4096,512]{1,0:T(8,128)(2,1)} %all-gather.5.cloned.1.call-done), kind=kOutput, calls=%fused_computation.44 | convolution fusion | flops 1073872896 | bytes 6553600 | tf_op jit(solution)/shard_map/dot_general | solution.py:88
  155.0 22.5 %all-gather = s32[16,1,512]{2,1,0:T(1,128)S(1)} all-gather(s32[1,1,512]{2,1,0:T(1,128)S(1)} %bitcast.107), channel_id=1, replica_groups=mesh['ctx'=4,'row'=4,'col_0'=2,'col_1'=8] {'ctx','row'}, dimensions={0}, use_global_device_ids=true | all-gather | bytes 34816 | tf_op jit(solution)/shard_map/all_gather | solution.py:124
  177.7 4.2 %fusion.28 = bf16[512,256]{0,1:T(8,128)(2,1)S(1)} fusion(bf16[512,4096]{0,1:T(8,128)(2,1)} %fusion.20, bf16[4096,512]{1,0:T(8,128)(2,1)} %all-gather.5.cloned.1.call-done), kind=kOutput, calls=%fused_computation.45 | convolution fusion | flops 1073872896 | bytes 6553600 | tf_op jit(solution)/shard_map/dot_general | solution.py:87
  182.1 28.0 %all-gather.7.cloned.1.call-done = bf16[8192,1,2,128]{3,0,2,1:T(8,128)(2,1)} async-done(((bf16[512,1,2,128]{3,0,2,1:T(8,128)(2,1)}), bf16[8192,1,2,128]{3,0,2,1:T(8,128)(2,1)}) %all-gather.7.cloned.1.call-update) | async-done | bytes 4194320 | tf_op jit(solution)/shard_map/all_gather | solution.py:123
  210.1 72.2 %while.13 = (s32[]{:T(128)}, f32[512,1,2,128]{0,3,2,1:T(8,128)S(1)}, bf16[16,512,1,2,128]{4,1,0,3,2:T(8,128)(2,1)}, s32[16]{0:T(128)S(1)}, s32[4]{0:T(128)S(1)},...) while((s32[]{:T(128)}, ...), condition=%wide.region_4.5_spmd.clone, body=%wide.region_2.4_spmd.clone.sunk | while | flops 274747904 | bytes 4743363 | solution.py:134
  213.4 1.2 fusion.45
  222.4 1.2 fusion.45
  226.9 1.2 fusion.45
  231.4 1.2 fusion.45
  235.9 1.2 fusion.45
  240.5 1.2 fusion.45
  245.0 1.2 fusion.45
  249.5 1.2 fusion.45
  254.0 1.2 fusion.45
  258.5 1.2 fusion.45
  263.0 1.2 fusion.45
  267.5 1.2 fusion.45
  272.1 1.2 fusion.45
  276.6 1.2 fusion.45
  281.1 1.2 fusion.45
  283.2 69.0 %all_to_all.16 = bf16[4,1024,256]{2,1,0:T(8,128)(2,1)S(1)} all-to-all(bf16[4,1024,256]{2,1,0:T(8,128)(2,1)S(1)} %broadcast_in_dim.70), channel_id=1, replica_groups=mesh['ctx'=4,'row'=4,'col_0'=2,'col_1'=8] {'row'}, dimensions={0} | all-to-all | bytes 4194304 | tf_op jit(solution)/shard_map/all_to_all | solution.py:50
  352.2 6.7 %all-gather.9.cloned.1.call-done = bf16[512,4096]{0,1:T(8,128)(2,1)} async-done(((bf16[512,256]{0,1:T(8,128)(2,1)}), bf16[512,4096]{0,1:T(8,128)(2,1)}) %all-gather.9.cloned.1.call-update) | async-done | bytes 4194320 | tf_op jit(solution)/shard_map/all_gather | solution.py:137
  358.9 4.2 %convolution_convert_fusion = bf16[512,256]{1,0:T(8,128)(2,1)} fusion(bf16[512,4096]{0,1:T(8,128)(2,1)} %all-gather.9.cloned.1.call-done, bf16[4096,256]{1,0:T(8,128)(2,1)S(1)} %bitcast.98), kind=kOutput, calls=%fused_computation.46 | convolution fusion | flops 1073872896 | bytes 6553600 | tf_op jit(solution)/shard_map/dot_general | solution.py:139
  (144 shorter events, 57.7 us)
Async XLA Ops:
  20.6 10.2 %copy-start.1 = (bf16[1024,256]{1,0:T(8,128)(2,1)S(1)}, bf16[1024,256]{1,0:T(8,128)(2,1)}, u32[]{:S(2)}) copy-start(bf16[1024,256]{1,0:T(8,128)(2,1)} %param.12) | copy-start | bytes 1572868
  20.6 104.0 %all-to-all-start.1 = ((bf16[8,2,512,256]{3,2,1,0:T(8,128)(2,1)}), bf16[8,2,512,256]{3,2,1,0:T(8,128)(2,1)}, u32[]{:S(2)}, u32[]{:S(2)}) async-start(bf16[8,2,512,256]{3,2,1,0:T(8,128)(2,1)} %stack.7), calls=%async_computation.1 | async-start | bytes 8388608 | tf_op jit(solution)/shard_map/all_to_all | solution.py:27
  29.2 120.7 %all-gather.5.cloned.1.call-start = ((), (), s32[]{:S(2)}) async-start(), calls=%async_computation.3 | async-start | bytes 5242880 | tf_op jit(solution)/shard_map/all_gather | solution.py:41
  32.0 178.1 %all-gather.7.cloned.1.call-start = ((), (), s32[]{:S(2)}) async-start(), calls=%async_computation.4 | async-start | bytes 4456448 | tf_op jit(solution)/shard_map/all_gather | solution.py:123
  149.9 5.1 %copy-start.2 = (s32[512]{0:T(512)S(1)}, s32[512]{0:T(512)}, u32[]{:S(2)}) copy-start(s32[512]{0:T(512)} %param.10) | copy-start | bytes 6148
  149.9 27.7 %copy-start.3 = (s32[4]{0:T(128)S(1)}, s32[4]{0:T(128)}, u32[]{:S(2)}) copy-start(s32[4]{0:T(128)} %param.11) | copy-start | bytes 52
  155.0 203.9 %all-gather.9.cloned.1.call-start = ((), (), s32[]{:S(2)}) async-start(), calls=%async_computation.5 | async-start | bytes 4456448 | tf_op jit(solution)/shard_map/all_gather | solution.py:137
  177.7 32.4 %copy-start.4 = (f32[2]{0:T(128)S(1)}, f32[2]{0:T(128)}, u32[]{:S(2)}) copy-start(f32[2]{0:T(128)} %param.14) | copy-start | bytes 28
  210.1 73.0 %copy-start = (bf16[1024,256]{1,0:T(8,128)(2,1)S(1)}, bf16[1024,256]{1,0:T(8,128)(2,1)}, u32[]{:S(2)}) copy-start(bf16[1024,256]{1,0:T(8,128)(2,1)} %param.15) | copy-start | bytes 1572868
Sparse Core Ops, SparseCore 0:
  32.1 42.5 all-gather.4
  155.1 54.9 all-gather.6
  283.2 75.6 all-gather.8
